TPU v7x, 32 devices: a whole 2x2x4 slice. The times are simulated.
32 devices in a mesh: lat: 8 (over z, y), lon: 4 (over x, core).
Axes of the slice: x: 2, y: 2, z: 4, core: 2. Of those that a mesh axis runs over, the one named last changes fastest.
Arguments:
- fields: bfloat16 [69, 128, 512], P(None, 'lat', 'lon'), may hold values from -6 to 6
- enc_kernel: bfloat16 [3, 3, 256, 69], replicated, may hold values from -0.25 to 0.25
- gen_kernel: bfloat16 [3, 3, 69, 256], replicated, may hold values from -0.125 to 0.125
- recon_grad: bfloat16 [69, 128, 512], P(None, 'lat', 'lon'), may hold values from -6 to 6
Outputs:
- rebuilt: bfloat16 [69, 128, 512], P(None, 'lat', 'lon')
- feat_grad: bfloat16 [256, 128, 512], P(None, 'lat', 'lon')
- enc_grad: float32 [3, 3, 256, 69], replicated
- gen_grad: float32 [3, 3, 69, 256], replicated
All inputs are finite; a program needn't handle non-finite values.
Results may differ from a plain program's by a relative error of at most 0.0085.
Values may be sent and summed in bfloat16 or wider, within the bound.
A program may use at most 64 MiB of HBM per device.

v0:
```python
import jax
import jax.numpy as jnp
from jax import lax
from jax.sharding import PartitionSpec as P


def extended(cells, sides, width, closed):
    for axis, dim in sides:
        count = lax.axis_size(axis)
        ends = count if closed else count - 1
        head = lax.slice_in_dim(cells, 0, width, axis=dim)
        tail = lax.slice_in_dim(cells, cells.shape[dim] - width, cells.shape[dim], axis=dim)
        cells = jnp.concatenate(
            [
                lax.ppermute(tail, axis, [(i, (i + 1) % count) for i in range(ends)]),
                cells,
                lax.ppermute(head, axis, [((i + 1) % count, i) for i in range(ends)]),
            ],
            axis=dim,
        )
    return cells


def from_behind(value, axis, steps):
    count = lax.axis_size(axis)
    pairs = [(source, (source + steps) % count) for source in range(count)]
    return lax.ppermute(value, axis, pairs)


def face_pad(source):
    lon_count = lax.axis_size("lon")
    widened = extended(source, (("lon", 2),), 1, True)
    edge_rows = jnp.concatenate([widened[:, :1], widened[:, -1:]], axis=1)
    pole_rows = from_behind(edge_rows, "lon", lon_count // 2)
    plain_pad = extended(widened, (("lat", 1),), 1, False)
    result = (plain_pad, pole_rows)
    return result


def with_poles(plain_pad, pole_rows):
    lat_index = lax.axis_index("lat")
    lat_count = lax.axis_size("lat")
    upper = jnp.where(lat_index == 0, pole_rows[:, :1], plain_pad[:, :1])
    lower = jnp.where(lat_index == lat_count - 1, pole_rows[:, 1:], plain_pad[:, -1:])
    return jnp.concatenate([upper, plain_pad[:, 1:-1], lower], axis=1)


def convolve(padded, kernel, height, width):
    running = None
    for row_tap in range(3):
        for col_tap in range(3):
            section = padded[:, row_tap : row_tap + height, col_tap : col_tap + width].reshape(
                padded.shape[0], height * width
            )
            product = jnp.dot(kernel[row_tap, col_tap], section, preferred_element_type=jnp.float32)
            running = product if running is None else running + product
    return running.reshape(kernel.shape[2], height, width)


def adjoint_conv(padded, kernel, height, width):
    running = None
    for row_tap in range(3):
        for col_tap in range(3):
            section = padded[
                :, 2 - row_tap : 2 - row_tap + height, 2 - col_tap : 2 - col_tap + width
            ].reshape(padded.shape[0], height * width)
            product = lax.dot_general(
                kernel[row_tap, col_tap],
                section,
                (((0,), (0,)), ((), ())),
                preferred_element_type=jnp.float32,
            )
            running = product if running is None else running + product
    return running.reshape(kernel.shape[3], height, width)


def pole_terms(pole_rows, kernel, width):
    terms = []
    for which, row_tap in ((0, 0), (1, 2)):
        running = None
        for col_tap in range(3):
            section = pole_rows[:, which, 2 - col_tap : 2 - col_tap + width]
            product = lax.dot_general(
                kernel[row_tap, col_tap],
                section,
                (((0,), (0,)), ((), ())),
                preferred_element_type=jnp.float32,
            )
            running = product if running is None else running + product
        terms.append(running)
    return (terms[0], terms[1])


def weight_grad(cotangent, padded, height, width):
    flat_cot = cotangent.reshape(cotangent.shape[0], height * width)
    taps = []
    for row_tap in range(3):
        row_list = []
        for col_tap in range(3):
            section = padded[:, row_tap : row_tap + height, col_tap : col_tap + width].reshape(
                padded.shape[0], height * width
            )
            row_list.append(
                lax.dot_general(
                    flat_cot, section, (((1,), (1,)), ((), ())), preferred_element_type=jnp.float32
                )
            )
        taps.append(jnp.stack(row_list))
    return jnp.stack(taps)


def sum_grads(enc_part, gen_part):
    summed = lax.psum((enc_part, gen_part), ("lat", "lon"))
    return summed


def on_device(fields, enc_kernel, gen_kernel, recon_grad):
    height = fields.shape[1]
    width = fields.shape[2]
    in_count = fields.shape[0]
    lat_index = lax.axis_index("lat")
    lat_count = lax.axis_size("lat")
    lon_count = lax.axis_size("lon")
    plain_pair, pole_pair = face_pad(jnp.concatenate([fields, recon_grad], axis=0))
    plain_in = plain_pair[:in_count]
    pole_in = pole_pair[:in_count]
    plain_cot = plain_pair[in_count:]
    pole_cot = pole_pair[in_count:]
    padded_in = with_poles(plain_in, pole_in)
    pre_act = convolve(padded_in, enc_kernel, height, width)
    hidden = jax.nn.silu(pre_act).astype(jnp.bfloat16)
    plain_hid, pole_hid = face_pad(hidden)
    padded_hid = with_poles(plain_hid, pole_hid)
    rebuilt = convolve(padded_hid, gen_kernel, height, width).astype(jnp.bfloat16)
    feat_f32 = adjoint_conv(plain_cot, gen_kernel, height, width)
    upper_term, lower_term = pole_terms(pole_cot, gen_kernel, width)
    feat_f32 = feat_f32.at[:, 0].add(jnp.where(lat_index == 0, upper_term, 0.0))
    feat_f32 = feat_f32.at[:, -1].add(jnp.where(lat_index == lat_count - 1, lower_term, 0.0))
    feat_grad = feat_f32.astype(jnp.bfloat16)
    logistic = jax.nn.sigmoid(pre_act)
    pre_grad = (
        feat_grad.astype(jnp.float32) * logistic * (1.0 + pre_act * (1.0 - logistic))
    ).astype(jnp.bfloat16)
    gen_part = weight_grad(recon_grad, padded_hid, height, width)
    enc_part = weight_grad(pre_grad, padded_in, height, width)
    enc_sum, gen_sum = sum_grads(enc_part, gen_part)
    norm_scale = 1.0 / jnp.sqrt(jnp.float32(height * lat_count * width * lon_count))
    return (rebuilt, feat_grad, enc_sum * norm_scale, gen_sum * norm_scale)


def solution(mesh):
    return jax.shard_map(
        on_device,
        mesh=mesh,
        in_specs=(P(None, "lat", "lon"), P(), P(), P(None, "lat", "lon")),
        out_specs=(P(None, "lat", "lon"), P(None, "lat", "lon"), P(), P()),
        check_vma=False,
    )
```

profile of v0, /device:TPU:0, one launch (start us, length us, event | category | flops | bytes accessed | tf_op | source)
XLA Modules:
  0.0 219.3 jit_solution(15706340045346851141)
XLA Ops:
  7.2 1.1 copy.90
  8.3 1.1 copy.91
  9.7 0.4 copy.93
  10.1 2.4 %collective-permute-start.1 = (bf16[138,16,1]{0,1,2:T(8,128)(2,1)S(1)}, bf16[138,16,1]{0,1,2:T(8,128)(2,1)S(1)}, u32[]{:S(2)}, u32[]{:S(2)}) collective-permute-start(bf16[138,16,1]{0,1,2:T(8,128)(2,1)S(1)} %copy.93), channel_id=1, source_target_pairs={{1,0},{2,1},{3,2},{0,3},{5,4},{6,5},{7,6},{4,7},{9,8},{10,9},{11,1... | collective-permute-start | bytes 13256 | tf_op jit(solution)/shard_map/ppermute | solution.py:17
  12.6 0.4 copy.92
  13.3 0.7 collective-permute-done.1
  14.3 1.8 collective-permute-done
  16.9 0.5 pad_maximum_fusion.17
  17.5 1.3 collective-permute-start.4
  18.8 4.7 %collective-permute-start.3 = (bf16[138,1,130]{2,0,1:T(8,128)(2,1)S(1)}, bf16[138,1,130]{2,0,1:T(8,128)(2,1)S(1)}, u32[]{:S(2)}, u32[]{:S(2)}) collective-permute-start(bf16[138,1,130]{2,0,1:T(8,128)(2,1)S(1)} %get-tuple-element.52), channel_id=1, source_target_pairs={{0,4},{4,8},{8,12},{12,16},{16,20},{20,24},{24,28},{1,5},{5,9},{9,... | collective-permute-start | bytes 107648 | tf_op jit(solution)/shard_map/ppermute | solution.py:15
  23.5 0.6 collective-permute-start.2
  24.5 0.8 pad_maximum_fusion.19
  25.4 0.9 pad_maximum_fusion.9
  27.4 0.6 copy-done.6
  27.9 0.5 fusion.55
  28.4 0.5 convolution_add_fusion.3
  28.9 0.5 convolution_add_fusion.2
  29.4 0.5 fusion.4
  29.9 0.5 convolution_add_fusion
  30.4 0.5 fusion.3
  30.9 0.5 fusion.2
  31.4 0.5 fusion.1
  31.9 0.5 fusion
  32.6 0.4 pad_maximum_fusion.25
  34.0 0.6 copy-done.8
  34.6 0.5 fusion.67
  35.0 0.5 convolution_add_fusion.7
  35.5 0.5 convolution_add_fusion.6
  36.0 0.5 fusion.9
  36.5 0.5 convolution_add_fusion.4
  37.0 0.5 fusion.8
  37.5 0.5 fusion.7
  38.0 0.5 fusion.6
  38.5 0.7 fusion.5
  39.2 1.5 fusion.23
  42.3 0.9 multiply_convert_fusion
  45.7 0.6 fusion.121
  47.0 1.7 collective-permute-start.6
  48.8 0.9 pad_maximum_fusion.3
  49.7 1.8 copy.144
  51.5 4.4 %collective-permute-start.8 = (bf16[256,1,130]{0,2,1:T(8,128)(2,1)S(1)}, bf16[256,1,130]{0,2,1:T(8,128)(2,1)S(1)}, u32[]{:S(2)}, u32[]{:S(2)}) collective-permute-start(bf16[256,1,130]{0,2,1:T(8,128)(2,1)S(1)} %get-tuple-element.65), channel_id=1, source_target_pairs={{0,4},{4,8},{8,12},{12,16},{16,20},{20,24},{24,28},{1,5},{5,9},{9,... | collective-permute-start | bytes 199688 | tf_op jit(solution)/shard_map/ppermute | solution.py:15
  55.9 1.3 collective-permute-start.9
  57.2 1.5 collective-permute-start.7
  58.7 0.6 pad_maximum_fusion.1
  60.0 3.3 %collective-permute-done.9 = bf16[256,1,130]{0,2,1:T(8,128)(2,1)S(1)} collective-permute-done((bf16[256,1,130]{0,2,1:T(8,128)(2,1)S(1)}, bf16[256,1,130]{0,2,1:T(8,128)(2,1)S(1)}, u32[]{:S(2)}, u32[]{:S(2)}) %collective-permute-start.9) | collective-permute-done | bytes 66592 | tf_op jit(solution)/shard_map/ppermute | solution.py:17
  63.2 0.7 maximum_maximum_fusion
  63.9 0.4 convolution_bitcast_fusion.14
  64.6 0.4 convolution_bitcast_fusion.15
  65.0 0.4 convolution_bitcast_fusion.8
  65.7 0.4 convolution_bitcast_fusion.9
  66.1 3.3 %fusion.119 = (bf16[256,16,128]{0,2,1:T(8,128)(2,1)}, bf16[256,16,128]{0,2,1:T(8,128)(2,1)S(1)}, bf16[256,16,128]{0,2,1:T(8,128)(2,1)S(1)}, bf16[256,16,128]{0,2...) fusion(bf16[256,17,130]{0,2,1:T(8,128)(2,1)S(1)} %get-tuple-element.64, ...), kind=kLoop, calls=%fused_computation.229 | loop fusion | bytes 12582912 | tf_op jit(solution)/shard_map/slice | solution.py:52
  69.4 2.0 fusion.38
  71.4 2.0 fusion.57
  73.5 0.9 pad_maximum_fusion.4
  74.4 2.0 convolution_add_fusion.13
  76.4 1.3 convolution_add_fusion.12
  77.7 1.2 fusion.10
  79.0 1.3 fusion.11
  80.3 1.2 convolution_add_fusion.9
  81.5 1.2 fusion.12
  82.8 0.7 slice.427
  83.5 125.0 %all-reduce.3.cloned.1.call-done = (f32[3,3,256,69]{2,3,1,0:T(8,128)}, f32[3,3,69,256]{3,2,1,0:T(8,128)}) async-done(((f32[3,3,256,69]{2,3,1,0:T(8,128)}, f32[3,3,69,256]{3,2,1,0:T(8,128)}), (f32[3,3,256,69]{2,3,1,0:T(8,128)}, f32[3,3,69,256]{3,2,1,0:T(8,128)})) %all-reduce.3.cloned.1.call-update) | async-done | bytes 1271824 | tf_op jit(solution)/shard_map/psum | solution.py:113
  208.5 2.0 broadcast_multiply_fusion.1
  210.5 2.0 broadcast_multiply_fusion
  (114 shorter events, 10.1 us)
Async XLA Ops:
  7.2 5.8 %copy-start.3 = (bf16[69,16,128]{2,1,0:T(8,128)(2,1)S(1)}, bf16[69,16,128]{2,1,0:T(8,128)(2,1)}, u32[]{:S(2)}) copy-start(bf16[69,16,128]{2,1,0:T(8,128)(2,1)} %param.8) | copy-start | bytes 847876
  7.2 201.4 %all-reduce.3.cloned.1.call-start = ((), (), s32[]{:S(2)}) async-start(), calls=%async_computation | async-start | bytes 2654208 | tf_op jit(solution)/shard_map/psum | solution.py:113
  8.3 4.7 %copy-start = (bf16[69,16,128]{2,1,0:T(8,128)(2,1)S(1)}, bf16[69,16,128]{2,1,0:T(8,128)(2,1)}, u32[]{:S(2)}) copy-start(bf16[69,16,128]{2,1,0:T(8,128)(2,1)} %param.11) | copy-start | bytes 847876
  10.1 3.8 %collective-permute-start.1 = (bf16[138,16,1]{0,1,2:T(8,128)(2,1)S(1)}, bf16[138,16,1]{0,1,2:T(8,128)(2,1)S(1)}, u32[]{:S(2)}, u32[]{:S(2)}) collective-permute-start(bf16[138,16,1]{0,1,2:T(8,128)(2,1)S(1)} %copy.93), channel_id=1, source_target_pairs={{1,0},{2,1},{3,2},{0,3},{5,4},{6,5},{7,6},{4,7},{9,8},{10,9},{11,1... | collective-permute-start | bytes 13256 | tf_op jit(solution)/shard_map/ppermute | solution.py:17
  12.9 3.1 %collective-permute-start = (bf16[138,16,1]{0,1,2:T(8,128)(2,1)S(1)}, bf16[138,16,1]{0,1,2:T(8,128)(2,1)S(1)}, u32[]{:S(2)}, u32[]{:S(2)}) collective-permute-start(bf16[138,16,1]{0,1,2:T(8,128)(2,1)S(1)} %copy.92), channel_id=1, source_target_pairs={{0,1},{1,2},{2,3},{3,0},{4,5},{5,6},{6,7},{7,4},{8,9},{9,10},{10,1... | collective-permute-start | bytes 13256 | tf_op jit(solution)/shard_map/ppermute | solution.py:15
  17.5 7.0 %collective-permute-start.4 = (bf16[138,1,130]{2,0,1:T(8,128)(2,1)S(1)}, bf16[138,1,130]{2,0,1:T(8,128)(2,1)S(1)}, u32[]{:S(2)}, u32[]{:S(2)}) collective-permute-start(bf16[138,1,130]{2,0,1:T(8,128)(2,1)S(1)} %get-tuple-element.51), channel_id=1, source_target_pairs={{4,0},{8,4},{12,8},{16,12},{20,16},{24,20},{28,24},{5,1},{9,5},{13... | collective-permute-start | bytes 107648 | tf_op jit(solution)/shard_map/ppermute | solution.py:17
  18.8 6.6 %collective-permute-start.3 = (bf16[138,1,130]{2,0,1:T(8,128)(2,1)S(1)}, bf16[138,1,130]{2,0,1:T(8,128)(2,1)S(1)}, u32[]{:S(2)}, u32[]{:S(2)}) collective-permute-start(bf16[138,1,130]{2,0,1:T(8,128)(2,1)S(1)} %get-tuple-element.52), channel_id=1, source_target_pairs={{0,4},{4,8},{8,12},{12,16},{16,20},{20,24},{24,28},{1,5},{5,9},{9,... | collective-permute-start | bytes 107648 | tf_op jit(solution)/shard_map/ppermute | solution.py:15
  23.5 9.0 %collective-permute-start.2 = (bf16[138,2,130]{2,0,1:T(8,128)(2,1)S(1)}, bf16[138,2,130]{2,0,1:T(8,128)(2,1)S(1)}, u32[]{:S(2)}, u32[]{:S(2)}) collective-permute-start(bf16[138,2,130]{2,0,1:T(8,128)(2,1)S(1)} %pad_maximum_fusion.29), channel_id=1, source_target_pairs={{0,2},{1,3},{2,0},{3,1},{4,6},{5,7},{6,4},{7,5},{8,10},{9,11},{10,... | collective-permute-start | bytes 215288 | tf_op jit(solution)/shard_map/ppermute | solution.py:27
  27.0 1.0 copy-start.6
  33.6 1.0 copy-start.8
  45.1 1.5 copy-start.4
  46.9 4.5 %collective-permute-start.5 = (bf16[256,16,1]{0,2,1:T(2,128)(2,1)}, bf16[256,16,1]{0,2,1:T(2,128)(2,1)S(1)}, u32[]{:S(2)}, u32[]{:S(2)}) collective-permute-start(bf16[256,16,1]{0,2,1:T(2,128)(2,1)} %get-tuple-element.69), channel_id=1, source_target_pairs={{0,1},{1,2},{2,3},{3,0},{4,5},{5,6},{6,7},{7,4},{8,9},{9,10},{10,1... | collective-permute-start | bytes 24584 | tf_op jit(solution)/shard_map/ppermute | solution.py:15
  47.0 4.5 %collective-permute-start.6 = (bf16[256,16,1]{0,2,1:T(2,128)(2,1)S(1)}, bf16[256,16,1]{0,2,1:T(2,128)(2,1)S(1)}, u32[]{:S(2)}, u32[]{:S(2)}) collective-permute-start(bf16[256,16,1]{0,2,1:T(2,128)(2,1)S(1)} %get-tuple-element.70), channel_id=1, source_target_pairs={{1,0},{2,1},{3,2},{0,3},{5,4},{6,5},{7,6},{4,7},{9,8},{10,9},{11,1... | collective-permute-start | bytes 24584 | tf_op jit(solution)/shard_map/ppermute | solution.py:17
  51.5 8.4 %collective-permute-start.8 = (bf16[256,1,130]{0,2,1:T(8,128)(2,1)S(1)}, bf16[256,1,130]{0,2,1:T(8,128)(2,1)S(1)}, u32[]{:S(2)}, u32[]{:S(2)}) collective-permute-start(bf16[256,1,130]{0,2,1:T(8,128)(2,1)S(1)} %get-tuple-element.65), channel_id=1, source_target_pairs={{0,4},{4,8},{8,12},{12,16},{16,20},{20,24},{24,28},{1,5},{5,9},{9,... | collective-permute-start | bytes 199688 | tf_op jit(solution)/shard_map/ppermute | solution.py:15
  55.9 7.3 %collective-permute-start.9 = (bf16[256,1,130]{0,2,1:T(8,128)(2,1)S(1)}, bf16[256,1,130]{0,2,1:T(8,128)(2,1)S(1)}, u32[]{:S(2)}, u32[]{:S(2)}) collective-permute-start(bf16[256,1,130]{0,2,1:T(8,128)(2,1)S(1)} %get-tuple-element.66), channel_id=1, source_target_pairs={{4,0},{8,4},{12,8},{16,12},{20,16},{24,20},{28,24},{5,1},{9,5},{13... | collective-permute-start | bytes 199688 | tf_op jit(solution)/shard_map/ppermute | solution.py:17
  57.2 6.0 %collective-permute-start.7 = (bf16[256,2,130]{0,2,1:T(8,128)(2,1)S(1)}, bf16[256,2,130]{0,2,1:T(8,128)(2,1)S(1)}, u32[]{:S(2)}, u32[]{:S(2)}) collective-permute-start(bf16[256,2,130]{0,2,1:T(8,128)(2,1)S(1)} %pad_maximum_fusion.30), channel_id=1, source_target_pairs={{0,2},{1,3},{2,0},{3,1},{4,6},{5,7},{6,4},{7,5},{8,10},{9,11},{10,... | collective-permute-start | bytes 399368 | tf_op jit(solution)/shard_map/ppermute | solution.py:27
  74.4 2.0 copy-start.1
  74.4 3.3 %copy-start.7 = (f32[2048,69]{0,1:T(8,128)S(1)}, f32[2048,69]{0,1:T(8,128)}, u32[]{:S(2)}) copy-start(f32[2048,69]{0,1:T(8,128)} %fusion.23) | copy-start | bytes 1695748
  76.4 2.5 %copy-start.5 = (f32[2048,69]{0,1:T(8,128)S(1)}, f32[2048,69]{0,1:T(8,128)}, u32[]{:S(2)}) copy-start(f32[2048,69]{0,1:T(8,128)} %fusion.38) | copy-start | bytes 1695748
  78.9 2.5 %copy-start.2 = (bf16[256,16,128]{0,2,1:T(8,128)(2,1)S(1)}, bf16[256,16,128]{0,2,1:T(8,128)(2,1)}, u32[]{:S(2)}) copy-start(bf16[256,16,128]{0,2,1:T(8,128)(2,1)} %get-tuple-element.53) | copy-start | bytes 3145732
Sparse Core Ops, SparseCore 0:
  74.5 133.9 all-reduce.2
where the time goes:
time: 220 us; the launch traced here: 219 us
  waiting for transfers between devices  131 us (60%)
  matrix products  30 us (14%)
  starting transfers between devices  18.1 us (8%)
  between operations  15 us (7%)
  local copies, waits for them, and re-layouts  13.7 us (6%)
  other arithmetic  11.7 us (5%)
    psum x1, waiting for transfers between devices, sum_grads(): summed = lax.psum((enc_part, gen_part), ('lat', 'lon'))  125 us
    dot_general x18, matrix products, convolve(): jnp.dot(kernel[row_tap, col_tap], section, preferred_element_type=jnp.flo...  18.4 us
    ppermute x4, starting transfers between devices, extended(): lax.ppermute(tail, axis, [(i, (i + 1) % count) for i in range(ends)])  9.17 us
    unnamed x58, local copies, waits for them, and re-layouts  6.96 us
    ppermute x4, starting transfers between devices, extended(): lax.ppermute(head, axis, [((i + 1) % count, i) for i in range(ends)])  6.75 us
    dot_general x18, matrix products, weight_grad(): lax.dot_general(flat_cot, section, (((1,), (1,)), ((), ())), preferred_el...  5.67 us
  transfers between devices with their start and end apart: 11, of which 4 were waited for; matrix products, arithmetic and copies ran while one was open for 10% of the time, Pallas kernels for 0%

commit v1 on v0

--- a/solution.py
+++ b/solution.py
@@ -110,7 +110,9 @@
 
 
 def sum_grads(enc_part, gen_part):
-    summed = lax.psum((enc_part, gen_part), ("lat", "lon"))
+    summed = (enc_part, gen_part)
+    for over in ("lon", "lat"):
+        summed = lax.psum(summed, over)
     return summed
 
 

time: 220 us -> 212 us (0.964)
  waiting for transfers between devices: 131 us -> 122 us
    psum x1 -> x2, waiting for transfers between devices: 125 us -> 116 us  [sum_grads(): summed = lax.psum(summed, over)]
    unnamed x58 -> x54, local copies, waits for them, and re-layouts: 6.96 us -> 6.95 us
  transfers between devices with their start and end apart: 11 -> 12, of which waited for: 4 -> 5; matrix products, arithmetic and copies ran while one was open for 10% -> 12% of each run, Pallas kernels for 0% -> 0%
where the time goes in v1:
time: 212 us; the launch traced here: 211 us
  waiting for transfers between devices  122 us (58%)
  matrix products  30.3 us (14%)
  starting transfers between devices  18.2 us (9%)
  between operations  15 us (7%)
  local copies, waits for them, and re-layouts  14.3 us (7%)
  other arithmetic  11.7 us (6%)
    psum x2, waiting for transfers between devices, sum_grads(): summed = lax.psum(summed, over)  116 us
    dot_general x18, matrix products, convolve(): jnp.dot(kernel[row_tap, col_tap], section, preferred_element_type=jnp.flo...  18.7 us
    ppermute x4, starting transfers between devices, extended(): lax.ppermute(tail, axis, [(i, (i + 1) % count) for i in range(ends)])  9.17 us
    unnamed x54, local copies, waits for them, and re-layouts  6.95 us
    ppermute x4, starting transfers between devices, extended(): lax.ppermute(head, axis, [((i + 1) % count, i) for i in range(ends)])  6.75 us
    dot_general x18, matrix products, weight_grad(): lax.dot_general(flat_cot, section, (((1,), (1,)), ((), ())), preferred_el...  5.66 us
    dot_general x9, matrix products, adjoint_conv(): lax.dot_general(kernel[row_tap, col_tap], section, (((0,), (0,)), ((), ()...  4.37 us
  transfers between devices with their start and end apart: 12, of which 5 were waited for; matrix products, arithmetic and copies ran while one was open for 12% of the time, Pallas kernels for 0%

profile of v1, /device:TPU:0, one launch (start us, length us, event | category | flops | bytes accessed | tf_op | source)
XLA Modules:
  0.0 211.2 jit_solution(4105708106610237733)
XLA Ops:
  7.2 1.1 copy.90
  8.3 1.1 copy.91
  9.7 0.4 copy.93
  10.1 2.4 %collective-permute-start.1 = (bf16[138,16,1]{0,1,2:T(8,128)(2,1)S(1)}, bf16[138,16,1]{0,1,2:T(8,128)(2,1)S(1)}, u32[]{:S(2)}, u32[]{:S(2)}) collective-permute-start(bf16[138,16,1]{0,1,2:T(8,128)(2,1)S(1)} %copy.93), channel_id=1, source_target_pairs={{1,0},{2,1},{3,2},{0,3},{5,4},{6,5},{7,6},{4,7},{9,8},{10,9},{11,1... | collective-permute-start | bytes 13256 | tf_op jit(solution)/shard_map/ppermute | solution.py:17
  13.3 0.7 collective-permute-done.1
  14.3 1.8 collective-permute-done
  16.9 0.5 pad_maximum_fusion.17
  17.5 1.3 collective-permute-start.4
  18.8 4.7 %collective-permute-start.3 = (bf16[138,1,130]{2,0,1:T(8,128)(2,1)S(1)}, bf16[138,1,130]{2,0,1:T(8,128)(2,1)S(1)}, u32[]{:S(2)}, u32[]{:S(2)}) collective-permute-start(bf16[138,1,130]{2,0,1:T(8,128)(2,1)S(1)} %get-tuple-element.54), channel_id=1, source_target_pairs={{0,4},{4,8},{8,12},{12,16},{16,20},{20,24},{24,28},{1,5},{5,9},{9,... | collective-permute-start | bytes 107648 | tf_op jit(solution)/shard_map/ppermute | solution.py:15
  23.5 0.6 collective-permute-start.2
  24.5 0.8 pad_maximum_fusion.19
  25.4 0.9 pad_maximum_fusion.9
  27.4 0.6 copy-done.5
  27.9 0.5 fusion.55
  28.4 0.5 convolution_add_fusion.3
  28.9 0.5 convolution_add_fusion.2
  29.4 0.5 fusion.4
  29.9 0.5 convolution_add_fusion
  30.4 0.5 fusion.3
  30.9 0.5 fusion.2
  31.4 0.5 fusion.1
  31.9 0.5 fusion
  32.6 0.4 pad_maximum_fusion.25
  34.0 0.6 copy-done.6
  34.6 0.5 fusion.67
  35.0 0.5 convolution_add_fusion.7
  35.5 0.5 convolution_add_fusion.6
  36.0 0.5 fusion.9
  36.5 0.5 convolution_add_fusion.4
  37.0 0.5 fusion.8
  37.5 0.5 fusion.7
  38.0 0.5 fusion.6
  38.5 0.7 fusion.5
  39.2 1.5 fusion.23
  42.3 0.9 multiply_convert_fusion
  45.7 0.6 fusion.121
  47.0 1.7 collective-permute-start.6
  48.8 0.9 pad_maximum_fusion.3
  49.7 1.8 copy.144
  51.5 4.4 %collective-permute-start.8 = (bf16[256,1,130]{0,2,1:T(8,128)(2,1)S(1)}, bf16[256,1,130]{0,2,1:T(8,128)(2,1)S(1)}, u32[]{:S(2)}, u32[]{:S(2)}) collective-permute-start(bf16[256,1,130]{0,2,1:T(8,128)(2,1)S(1)} %get-tuple-element.67), channel_id=1, source_target_pairs={{0,4},{4,8},{8,12},{12,16},{16,20},{20,24},{24,28},{1,5},{5,9},{9,... | collective-permute-start | bytes 199688 | tf_op jit(solution)/shard_map/ppermute | solution.py:15
  55.9 1.3 collective-permute-start.9
  57.2 1.5 collective-permute-start.7
  58.7 0.6 pad_maximum_fusion.1
  60.0 3.3 %collective-permute-done.9 = bf16[256,1,130]{0,2,1:T(8,128)(2,1)S(1)} collective-permute-done((bf16[256,1,130]{0,2,1:T(8,128)(2,1)S(1)}, bf16[256,1,130]{0,2,1:T(8,128)(2,1)S(1)}, u32[]{:S(2)}, u32[]{:S(2)}) %collective-permute-start.9) | collective-permute-done | bytes 66592 | tf_op jit(solution)/shard_map/ppermute | solution.py:17
  63.2 0.7 maximum_maximum_fusion
  63.9 0.4 convolution_bitcast_fusion.14
  64.6 0.4 convolution_bitcast_fusion.15
  65.0 0.4 convolution_bitcast_fusion.8
  65.7 0.4 convolution_bitcast_fusion.9
  66.1 3.9 %fusion.119 = (bf16[256,16,128]{0,2,1:T(8,128)(2,1)}, bf16[256,16,128]{0,2,1:T(8,128)(2,1)S(1)}, bf16[256,16,128]{0,2,1:T(8,128)(2,1)}, bf16[256,16,128]{0,2,1:T...) fusion(bf16[256,17,130]{0,2,1:T(8,128)(2,1)S(1)} %get-tuple-element.66, ...), kind=kLoop, calls=%fused_computation.229 | loop fusion | bytes 12582912 | tf_op jit(solution)/shard_map/slice | solution.py:52
  70.1 0.9 pad_maximum_fusion.4
  71.0 1.7 fusion.57
  72.8 1.7 convolution_add_fusion.13
  74.5 2.0 convolution_add_fusion.12
  76.5 36.5 %all-reduce.7.cloned.1.call-done = (f32[3,3,256,69]{2,3,1,0:T(8,128)}, f32[3,3,69,256]{3,2,1,0:T(8,128)}) async-done(((f32[3,3,256,69]{2,3,1,0:T(8,128)}, f32[3,3,69,256]{3,2,1,0:T(8,128)}), (f32[3,3,256,69]{2,3,1,0:T(8,128)}, f32[3,3,69,256]{3,2,1,0:T(8,128)})) %all-reduce.7.cloned.1.call-update) | async-done | bytes 1271824 | tf_op jit(solution)/shard_map/psum | solution.py:115
  113.0 1.7 fusion.38
  114.7 1.7 fusion.10
  116.4 1.3 fusion.11
  117.7 1.2 convolution_add_fusion.9
  118.9 1.2 fusion.12
  120.2 0.7 slice.427
  120.9 79.4 %all-reduce.5.cloned.1.call-done = (f32[3,3,256,69]{2,3,1,0:T(8,128)}, f32[3,3,69,256]{3,2,1,0:T(8,128)}) async-done(((f32[3,3,256,69]{2,3,1,0:T(8,128)}, f32[3,3,69,256]{3,2,1,0:T(8,128)}), (f32[3,3,256,69]{2,3,1,0:T(8,128)}, f32[3,3,69,256]{3,2,1,0:T(8,128)})) %all-reduce.5.cloned.1.call-update) | async-done | bytes 1271824 | tf_op jit(solution)/shard_map/psum | solution.py:115
  200.4 2.0 broadcast_multiply_fusion.1
  202.4 2.0 broadcast_multiply_fusion
  (113 shorter events, 10.6 us)
Async XLA Ops:
  7.2 5.8 %copy-start.3 = (bf16[69,16,128]{2,1,0:T(8,128)(2,1)S(1)}, bf16[69,16,128]{2,1,0:T(8,128)(2,1)}, u32[]{:S(2)}) copy-start(bf16[69,16,128]{2,1,0:T(8,128)(2,1)} %param.8) | copy-start | bytes 847876
  7.2 105.8 %all-reduce.7.cloned.1.call-start = ((), (), s32[]{:S(2)}) async-start(), calls=%async_computation.1 | async-start | bytes 2654208 | tf_op jit(solution)/shard_map/psum | solution.py:115
  8.3 4.7 %copy-start = (bf16[69,16,128]{2,1,0:T(8,128)(2,1)S(1)}, bf16[69,16,128]{2,1,0:T(8,128)(2,1)}, u32[]{:S(2)}) copy-start(bf16[69,16,128]{2,1,0:T(8,128)(2,1)} %param.11) | copy-start | bytes 847876
  10.1 3.8 %collective-permute-start.1 = (bf16[138,16,1]{0,1,2:T(8,128)(2,1)S(1)}, bf16[138,16,1]{0,1,2:T(8,128)(2,1)S(1)}, u32[]{:S(2)}, u32[]{:S(2)}) collective-permute-start(bf16[138,16,1]{0,1,2:T(8,128)(2,1)S(1)} %copy.93), channel_id=1, source_target_pairs={{1,0},{2,1},{3,2},{0,3},{5,4},{6,5},{7,6},{4,7},{9,8},{10,9},{11,1... | collective-permute-start | bytes 13256 | tf_op jit(solution)/shard_map/ppermute | solution.py:17
  12.9 3.1 %collective-permute-start = (bf16[138,16,1]{0,1,2:T(8,128)(2,1)S(1)}, bf16[138,16,1]{0,1,2:T(8,128)(2,1)S(1)}, u32[]{:S(2)}, u32[]{:S(2)}) collective-permute-start(bf16[138,16,1]{0,1,2:T(8,128)(2,1)S(1)} %copy.92), channel_id=1, source_target_pairs={{0,1},{1,2},{2,3},{3,0},{4,5},{5,6},{6,7},{7,4},{8,9},{9,10},{10,1... | collective-permute-start | bytes 13256 | tf_op jit(solution)/shard_map/ppermute | solution.py:15
  17.5 7.0 %collective-permute-start.4 = (bf16[138,1,130]{2,0,1:T(8,128)(2,1)S(1)}, bf16[138,1,130]{2,0,1:T(8,128)(2,1)S(1)}, u32[]{:S(2)}, u32[]{:S(2)}) collective-permute-start(bf16[138,1,130]{2,0,1:T(8,128)(2,1)S(1)} %get-tuple-element.53), channel_id=1, source_target_pairs={{4,0},{8,4},{12,8},{16,12},{20,16},{24,20},{28,24},{5,1},{9,5},{13... | collective-permute-start | bytes 107648 | tf_op jit(solution)/shard_map/ppermute | solution.py:17
  18.8 6.6 %collective-permute-start.3 = (bf16[138,1,130]{2,0,1:T(8,128)(2,1)S(1)}, bf16[138,1,130]{2,0,1:T(8,128)(2,1)S(1)}, u32[]{:S(2)}, u32[]{:S(2)}) collective-permute-start(bf16[138,1,130]{2,0,1:T(8,128)(2,1)S(1)} %get-tuple-element.54), channel_id=1, source_target_pairs={{0,4},{4,8},{8,12},{12,16},{16,20},{20,24},{24,28},{1,5},{5,9},{9,... | collective-permute-start | bytes 107648 | tf_op jit(solution)/shard_map/ppermute | solution.py:15
  23.5 9.0 %collective-permute-start.2 = (bf16[138,2,130]{2,0,1:T(8,128)(2,1)S(1)}, bf16[138,2,130]{2,0,1:T(8,128)(2,1)S(1)}, u32[]{:S(2)}, u32[]{:S(2)}) collective-permute-start(bf16[138,2,130]{2,0,1:T(8,128)(2,1)S(1)} %pad_maximum_fusion.29), channel_id=1, source_target_pairs={{0,2},{1,3},{2,0},{3,1},{4,6},{5,7},{6,4},{7,5},{8,10},{9,11},{10,... | collective-permute-start | bytes 215288 | tf_op jit(solution)/shard_map/ppermute | solution.py:27
  27.0 1.0 copy-start.5
  33.6 1.0 copy-start.6
  45.1 1.5 copy-start.4
  46.9 4.5 %collective-permute-start.5 = (bf16[256,16,1]{0,2,1:T(2,128)(2,1)}, bf16[256,16,1]{0,2,1:T(2,128)(2,1)S(1)}, u32[]{:S(2)}, u32[]{:S(2)}) collective-permute-start(bf16[256,16,1]{0,2,1:T(2,128)(2,1)} %get-tuple-element.71), channel_id=1, source_target_pairs={{0,1},{1,2},{2,3},{3,0},{4,5},{5,6},{6,7},{7,4},{8,9},{9,10},{10,1... | collective-permute-start | bytes 24584 | tf_op jit(solution)/shard_map/ppermute | solution.py:15
  47.0 4.5 %collective-permute-start.6 = (bf16[256,16,1]{0,2,1:T(2,128)(2,1)S(1)}, bf16[256,16,1]{0,2,1:T(2,128)(2,1)S(1)}, u32[]{:S(2)}, u32[]{:S(2)}) collective-permute-start(bf16[256,16,1]{0,2,1:T(2,128)(2,1)S(1)} %get-tuple-element.72), channel_id=1, source_target_pairs={{1,0},{2,1},{3,2},{0,3},{5,4},{6,5},{7,6},{4,7},{9,8},{10,9},{11,1... | collective-permute-start | bytes 24584 | tf_op jit(solution)/shard_map/ppermute | solution.py:17
  51.5 8.4 %collective-permute-start.8 = (bf16[256,1,130]{0,2,1:T(8,128)(2,1)S(1)}, bf16[256,1,130]{0,2,1:T(8,128)(2,1)S(1)}, u32[]{:S(2)}, u32[]{:S(2)}) collective-permute-start(bf16[256,1,130]{0,2,1:T(8,128)(2,1)S(1)} %get-tuple-element.67), channel_id=1, source_target_pairs={{0,4},{4,8},{8,12},{12,16},{16,20},{20,24},{24,28},{1,5},{5,9},{9,... | collective-permute-start | bytes 199688 | tf_op jit(solution)/shard_map/ppermute | solution.py:15
  55.9 7.3 %collective-permute-start.9 = (bf16[256,1,130]{0,2,1:T(8,128)(2,1)S(1)}, bf16[256,1,130]{0,2,1:T(8,128)(2,1)S(1)}, u32[]{:S(2)}, u32[]{:S(2)}) collective-permute-start(bf16[256,1,130]{0,2,1:T(8,128)(2,1)S(1)} %get-tuple-element.68), channel_id=1, source_target_pairs={{4,0},{8,4},{12,8},{16,12},{20,16},{24,20},{28,24},{5,1},{9,5},{13... | collective-permute-start | bytes 199688 | tf_op jit(solution)/shard_map/ppermute | solution.py:17
  57.2 6.0 %collective-permute-start.7 = (bf16[256,2,130]{0,2,1:T(8,128)(2,1)S(1)}, bf16[256,2,130]{0,2,1:T(8,128)(2,1)S(1)}, u32[]{:S(2)}, u32[]{:S(2)}) collective-permute-start(bf16[256,2,130]{0,2,1:T(8,128)(2,1)S(1)} %pad_maximum_fusion.30), channel_id=1, source_target_pairs={{0,2},{1,3},{2,0},{3,1},{4,6},{5,7},{6,4},{7,5},{8,10},{9,11},{10,... | collective-permute-start | bytes 399368 | tf_op jit(solution)/shard_map/ppermute | solution.py:27
  71.0 129.4 %all-reduce.5.cloned.1.call-start = ((), (), s32[]{:S(2)}) async-start(), calls=%async_computation | async-start | bytes 2654208 | tf_op jit(solution)/shard_map/psum | solution.py:115
  71.0 3.4 %copy-start.1 = (bf16[256,16,128]{0,2,1:T(8,128)(2,1)S(1)}, bf16[256,16,128]{0,2,1:T(8,128)(2,1)}, u32[]{:S(2)}) copy-start(bf16[256,16,128]{0,2,1:T(8,128)(2,1)} %get-tuple-element.90) | copy-start | bytes 3145732
  116.4 2.5 %copy-start.2 = (bf16[256,16,128]{0,2,1:T(8,128)(2,1)S(1)}, bf16[256,16,128]{0,2,1:T(8,128)(2,1)}, u32[]{:S(2)}) copy-start(bf16[256,16,128]{0,2,1:T(8,128)(2,1)} %get-tuple-element.55) | copy-start | bytes 3145732
Sparse Core Ops, SparseCore 0:
  71.1 41.8 all-reduce.6
  116.6 83.7 all-reduce.4
